TPU v7x, 512 devices: a whole 4x8x8 slice. The times are simulated.
512 devices in a mesh: blk: 128 (over z, y, x_lo), rep: 4 (over x_hi, core).
Axes of the slice: x: 4 (x_hi: 2, x_lo: 2; x = x_hi * 2 + x_lo), y: 8, z: 8, core: 2. Of those that a mesh axis runs over, the one named last changes fastest.
Arguments:
- left_emb: float32 [32768, 256], P('blk'), may hold values from -6 to 6
- left_state: float32 [32768], P('blk'), may hold values from 0.3 to 30
- right_emb: float32 [32768, 256], P('blk'), may hold values from -8 to 8
- right_state: float32 [32768], P('blk'), may hold values from 0.3 to 30
- relation: float32 [2, 256, 256], replicated, may hold values from -0.375 to 0.375
- relation_state: float32 [2, 256, 256], replicated, may hold values from 5242.88 to 524288
- edge_src: int32 [128, 4, 2, 2, 512], P('blk', 'rep'), may hold values from 0 to 255
- edge_dst: int32 [128, 4, 2, 2, 512], P('blk', 'rep'), may hold values from 0 to 255
- edge_rel: int32 [128, 4, 2, 2, 512], P('blk', 'rep'), may hold values from 0 to 1
- negatives: int32 [128, 4, 2, 2, 512], P('blk', 'rep'), may hold values from 0 to 255
- batch_counts: int32 [128, 4, 2], P('blk', 'rep'), may hold values from 0 to 2, as said below
Outputs:
- left_new: float32 [32768, 256], P('blk')
- left_state_new: float32 [32768], P('blk')
- right_new: float32 [32768, 256], P('blk')
- right_state_new: float32 [32768], P('blk')
- relation_new: float32 [2, 256, 256], replicated
- relation_state_new: float32 [2, 256, 256], replicated
Inputs may be any that keep to these rules, and one draw needn't show every extreme that they name: `batch_counts`: in each bucket the live edge batches of the 4 devices of one blk index number at most 4; in every draw some bucket has exactly that many, with some device at 2.
All inputs are finite; a program needn't handle non-finite values.
Results may differ from a plain program's by a relative error of at most 0.035.
Values sent between devices are 32-bit elements; how exact they have to be, the bound alone decides.
No kernel may reach another device: no remote copies, remote signals or barrier semaphores. Data moves between devices by JAX's collectives and lax.ppermute only.
A program may use at most 64 MiB of HBM per device.

v0:
```python
import jax
import jax.numpy as jnp
from jax import lax
from jax.sharding import PartitionSpec as P

learn_rate = 0.1


def from_behind(block, axis, distance):
    devices = range(lax.axis_size(axis))
    route = [((i - distance) % len(devices), i) for i in devices]
    return lax.ppermute(block, axis, route)


def batch_terms(query_table, right_bf, src_row, dst_row, rel_row, neg_row, live_flag):
    queries = query_table[rel_row, src_row]
    pos_rows = right_bf[dst_row]
    neg_rows = right_bf[neg_row]
    pos_score = jnp.sum(queries.astype(jnp.float32) * pos_rows.astype(jnp.float32), axis=-1)
    neg_score = lax.dot_general(
        queries, neg_rows, (((1,), (1,)), ((), ())), preferred_element_type=jnp.float32
    )
    row_top = jnp.maximum(jnp.max(neg_score, axis=1), pos_score)
    pos_exp = jnp.exp(pos_score - row_top)
    neg_exp = jnp.exp(neg_score - row_top[:, None])
    row_total = pos_exp + jnp.sum(neg_exp, axis=1)
    pos_weight = (pos_exp / row_total - 1.0) * live_flag
    weights = (neg_exp / row_total[:, None] * live_flag).astype(jnp.bfloat16)
    query_grad = jnp.dot(weights, neg_rows, preferred_element_type=jnp.float32) + pos_weight[
        :, None
    ] * pos_rows.astype(jnp.float32)
    neg_grad = lax.dot_general(
        weights, queries, (((0,), (0,)), ((), ())), preferred_element_type=jnp.float32
    )
    pos_grad = pos_weight[:, None] * queries.astype(jnp.float32)
    return (query_grad, neg_grad, pos_grad)


def bucket_terms(left_rows, right_rows, operator_bf, sources, targets, relations, negs, live_flags):
    left_bf = left_rows.astype(jnp.bfloat16)
    right_bf = right_rows.astype(jnp.bfloat16)
    query_table = jnp.einsum(
        "nd,rkd->rnk", left_bf, operator_bf, preferred_element_type=jnp.float32
    ).astype(jnp.bfloat16)
    nrel, rows, width = query_table.shape

    def step(position, carry):
        table_grad, right_grad = carry
        src_row = lax.dynamic_index_in_dim(sources, position, 0, keepdims=False)
        dst_row = lax.dynamic_index_in_dim(targets, position, 0, keepdims=False)
        rel_row = lax.dynamic_index_in_dim(relations, position, 0, keepdims=False)
        neg_row = lax.dynamic_index_in_dim(negs, position, 0, keepdims=False)
        live_flag = lax.dynamic_index_in_dim(live_flags, position, 0, keepdims=False)
        query_grad, neg_grad, pos_grad = batch_terms(
            query_table, right_bf, src_row, dst_row, rel_row, neg_row, live_flag
        )
        table_grad = table_grad.at[rel_row, src_row].add(query_grad)
        right_grad = right_grad.at[neg_row].add(neg_grad).at[dst_row].add(pos_grad)
        return (table_grad, right_grad)

    start = (jnp.zeros((nrel, rows, width), jnp.float32), jnp.zeros((rows, width), jnp.float32))
    table_grad, right_grad = lax.fori_loop(0, sources.shape[0], step, start)
    table_bf = table_grad.astype(jnp.bfloat16)
    left_grad = jnp.einsum("rnk,rkd->nd", table_bf, operator_bf, preferred_element_type=jnp.float32)
    operator_grad = jnp.einsum("rnk,nd->rkd", table_bf, left_bf, preferred_element_type=jnp.float32)
    return (left_grad, right_grad, operator_grad)


def row_update(embedding, accum, gradient):
    accum_next = accum + jnp.mean(gradient * gradient, axis=-1)
    return (embedding - learn_rate * gradient / jnp.sqrt(accum_next)[:, None], accum_next)


def body(
    left_emb,
    left_state,
    right_emb,
    right_state,
    relation,
    relation_state,
    edge_src,
    edge_dst,
    edge_rel,
    negatives,
    batch_counts,
):
    operator_bf = relation.astype(jnp.bfloat16)
    nbatch = edge_src.shape[3]
    left_rows, left_accum = (left_emb, left_state)
    right_rows, right_accum = (right_emb, right_state)
    operator_total = jnp.zeros(relation.shape, jnp.float32)
    for bucket in range(2):
        sources = edge_src[0, 0, bucket]
        targets = edge_dst[0, 0, bucket]
        relations = edge_rel[0, 0, bucket]
        negs = negatives[0, 0, bucket]
        live_flags = (jnp.arange(nbatch) < batch_counts[0, 0, bucket]).astype(jnp.float32)
        left_grad, right_grad, operator_grad = bucket_terms(
            left_rows, right_rows, operator_bf, sources, targets, relations, negs, live_flags
        )
        operator_total = operator_total + lax.psum(operator_grad, ("blk", "rep"))
        left_sum, right_sum = lax.psum((left_grad, right_grad), "rep")
        left_rows, left_accum = row_update(left_rows, left_accum, left_sum)
        right_rows, right_accum = row_update(right_rows, right_accum, right_sum)
        if bucket == 0:
            left_rows, left_accum = from_behind((left_rows, left_accum), "blk", 1)
    relation_state_new = relation_state + operator_total * operator_total
    relation_new = relation - learn_rate * operator_total / jnp.sqrt(relation_state_new)
    return (left_rows, left_accum, right_rows, right_accum, relation_new, relation_state_new)


def solution(mesh):
    in_specs = (
        P("blk", None),
        P("blk"),
        P("blk", None),
        P("blk"),
        P(),
        P(),
        P("blk", "rep", None, None, None),
        P("blk", "rep", None, None, None),
        P("blk", "rep", None, None, None),
        P("blk", "rep", None, None, None),
        P("blk", "rep", None),
    )
    out_specs = (P("blk", None), P("blk"), P("blk", None), P("blk"), P(), P())
    return jax.shard_map(body, mesh=mesh, in_specs=in_specs, out_specs=out_specs, check_vma=False)
```

profile of v0, /device:TPU:1, one launch (start us, length us, event | category | flops | bytes accessed | tf_op | source)
XLA Modules:
  0.0 608.4 jit_solution(12801148130178979247)
XLA Ops:
  14.1 91.3 %while.34 = (s32[]{:T(128)}, f32[2,256,256]{2,1,0:T(8,128)S(1)}, f32[256,256]{1,0:T(8,128)S(1)}, s32[2,512]{1,0:T(2,128)}, s32[2,512]{1,0:T(2,128)}, /*index=5*/...) while((s32[]{:T(128)}, f32[2,256,256]{2,1,0:T(8,128)S(1)}, ...), condition=%wide.region_7.8_spmd, body=%wide.region_0.7_spmd.sunk | while | flops 406075392 | bytes 12953801 | solution.py:62
  20.7 3.2 gather_fusion
  26.3 26.1 %scatter_fusion = f32[2,256,256]{2,1,0:T(8,128)S(1)} fusion(f32[2,256,256]{2,1,0:T(8,128)S(1)} %get-tuple-element.764, s32[512]{0:T(512)S(1)} %bitcast.154, f32[512,256]{1,0:T(8,128)S(1)} %convolution_add_fusion.5), kind=kCustom, calls=%fused_computation.6.clone.1 | custom fusion | flops 131072 | bytes 1576960 | tf_op jit(solution)/shard_map/while/body/eval_jaxpr/scatter-add | solution.py:57
  52.7 3.4 scatter_fusion.1
  56.1 3.6 scatter_custom_fusion.19
  66.3 3.2 gather_fusion
  71.9 26.1 %scatter_fusion = f32[2,256,256]{2,1,0:T(8,128)S(1)} fusion(f32[2,256,256]{2,1,0:T(8,128)S(1)} %get-tuple-element.764, s32[512]{0:T(512)S(1)} %bitcast.154, f32[512,256]{1,0:T(8,128)S(1)} %convolution_add_fusion.5), kind=kCustom, calls=%fused_computation.6.clone.1 | custom fusion | flops 131072 | bytes 1576960 | tf_op jit(solution)/shard_map/while/body/eval_jaxpr/scatter-add | solution.py:57
  98.3 3.4 scatter_fusion.1
  101.8 3.6 scatter_custom_fusion.19
  108.1 57.2 %all-reduce.10.cloned.1.call-done = (f32[256,256]{1,0:T(8,128)}, f32[256,256]{1,0:T(8,128)}) async-done(((f32[256,256]{1,0:T(8,128)}, f32[256,256]{1,0:T(8,128)}), (f32[256,256]{1,0:T(8,128)}, f32[256,256]{1,0:T(8,128)})) %all-reduce.10.cloned.1.call-update) | async-done | bytes 524304 | tf_op jit(solution)/shard_map/psum | solution.py:102
  167.8 2.5 collective-permute-start
  170.9 11.4 %collective-permute-done = f32[256,256]{1,0:T(8,128)S(1)} collective-permute-done((f32[256,256]{1,0:T(8,128)S(1)}, f32[256,256]{1,0:T(8,128)S(1)}, u32[]{:S(2)}, u32[]{:S(2)}) %collective-permute-start) | collective-permute-done | bytes 262176 | tf_op jit(solution)/shard_map/ppermute | solution.py:12
  182.7 91.3 %while.35 = (s32[]{:T(128)}, f32[2,256,256]{2,1,0:T(8,128)S(1)}, f32[256,256]{1,0:T(8,128)S(1)}, s32[2,512]{1,0:T(2,128)}, s32[2,512]{1,0:T(2,128)}, /*index=5*/...) while((s32[]{:T(128)}, f32[2,256,256]{2,1,0:T(8,128)S(1)}, ...), condition=%wide.region_19.20_spmd, body=%wide.region_12.19_spmd.sunk | while | flops 406075392 | bytes 12921097 | solution.py:62
  189.2 3.2 gather_fusion.3
  194.9 26.1 %scatter_fusion.2 = f32[2,256,256]{2,1,0:T(8,128)S(1)} fusion(f32[2,256,256]{2,1,0:T(8,128)S(1)} %get-tuple-element.797, s32[512]{0:T(512)S(1)} %bitcast.155, f32[512,256]{1,0:T(8,128)S(1)} %convolution_add_fusion.6), kind=kCustom, calls=%fused_computation.9.clone.1 | custom fusion | flops 131072 | bytes 1576960 | tf_op jit(solution)/shard_map/while/body/eval_jaxpr/scatter-add | solution.py:57
  221.3 3.4 scatter_fusion.3
  224.8 3.6 scatter_custom_fusion.23
  234.8 3.2 gather_fusion.3
  240.6 26.1 %scatter_fusion.2 = f32[2,256,256]{2,1,0:T(8,128)S(1)} fusion(f32[2,256,256]{2,1,0:T(8,128)S(1)} %get-tuple-element.797, s32[512]{0:T(512)S(1)} %bitcast.155, f32[512,256]{1,0:T(8,128)S(1)} %convolution_add_fusion.6), kind=kCustom, calls=%fused_computation.9.clone.1 | custom fusion | flops 131072 | bytes 1576960 | tf_op jit(solution)/shard_map/while/body/eval_jaxpr/scatter-add | solution.py:57
  267.0 3.4 scatter_fusion.3
  270.5 3.6 scatter_custom_fusion.23
  274.1 2.2 convolution_add_fusion.2
  280.0 262.9 %all-reduce.6.cloned.1.call-done = f32[2,256,256]{2,1,0:T(8,128)} async-done(((f32[2,256,256]{2,1,0:T(8,128)}), f32[2,256,256]{2,1,0:T(8,128)}) %all-reduce.6.cloned.1.call-update) | async-done | bytes 524304 | tf_op jit(solution)/shard_map/psum | solution.py:101
  545.0 51.2 %all-reduce.8.cloned.1.call-done = (f32[256,256]{1,0:T(8,128)}, f32[256,256]{1,0:T(8,128)}) async-done(((f32[256,256]{1,0:T(8,128)}, f32[256,256]{1,0:T(8,128)}), (f32[256,256]{1,0:T(8,128)}, f32[256,256]{1,0:T(8,128)})) %all-reduce.8.cloned.1.call-update) | async-done | bytes 524304 | tf_op jit(solution)/shard_map/psum | solution.py:102
  (162 shorter events, 61.3 us)
Async XLA Ops:
  7.2 158.1 %all-reduce.10.cloned.1.call-start = ((), (), s32[]{:S(2)}) async-start(), calls=%async_computation.2 | async-start | bytes 1048576 | tf_op jit(solution)/shard_map/psum | solution.py:102
  10.6 1.1 copy-start.2
  14.1 1.2 copy-start.11
  56.1 3.6 copy-start.12
  59.7 1.2 copy-start.11
  101.8 3.6 copy-start.12
  106.3 436.5 %all-reduce.6.cloned.1.call-start = ((), (), s32[]{:S(2)}) async-start(), calls=%async_computation | async-start | bytes 1048576 | tf_op jit(solution)/shard_map/psum | solution.py:101
  165.3 1.1 copy-start.9
  166.4 3.9 copy-start.13
  167.7 2.7 copy-start.21
  167.7 2.7 copy-start.3
  167.7 2.7 copy-start.5
  167.8 14.6 %collective-permute-start = (f32[256,256]{1,0:T(8,128)S(1)}, f32[256,256]{1,0:T(8,128)S(1)}, u32[]{:S(2)}, u32[]{:S(2)}) collective-permute-start(f32[256,256]{1,0:T(8,128)S(1)} %divide_subtract_fusion.3), channel_id=1, source_target_pairs={{508,0},{0,4},{4,8},{8,12},{12,16},{16,20},{20,24},{24,28},{28,32}... | collective-permute-start | bytes 786440 | tf_op jit(solution)/shard_map/ppermute | solution.py:12
  224.8 3.6 copy-start.27
  270.4 3.6 copy-start.27
  274.1 2.2 copy-start
  276.3 319.9 %all-reduce.8.cloned.1.call-start = ((), (), s32[]{:S(2)}) async-start(), calls=%async_computation.1 | async-start | bytes 1048576 | tf_op jit(solution)/shard_map/psum | solution.py:102
  276.4 266.5 %copy-start.10 = (f32[2,256,256]{2,1,0:T(8,128)S(1)}, f32[2,256,256]{2,1,0:T(8,128)}, u32[]{:S(2)}) copy-start(f32[2,256,256]{2,1,0:T(8,128)} %param.20) | copy-start | bytes 1572868
  277.3 265.6 %copy-start.7 = (f32[2,256,256]{2,1,0:T(8,128)S(1)}, f32[2,256,256]{2,1,0:T(8,128)}, u32[]{:S(2)}) copy-start(f32[2,256,256]{2,1,0:T(8,128)} %param.19) | copy-start | bytes 1572868
  278.1 322.5 %collective-permute-start.1 = (f32[256]{0:T(256)S(1)}, f32[256]{0:T(256)S(1)}, u32[]{:S(2)}, u32[]{:S(2)}) collective-permute-start(f32[256]{0:T(256)S(1)} %copy-done.25), channel_id=1, source_target_pairs={{508,0},{0,4},{4,8},{8,12},{12,16},{16,20},{20,24},{24,28},{28,32}... | collective-permute-start | bytes 3080 | tf_op jit(solution)/shard_map/ppermute | solution.py:12
  542.9 55.0 %copy-start.6 = (f32[256,256]{1,0:T(8,128)S(1)}, f32[256,256]{1,0:T(8,128)}, u32[]{:S(2)}) copy-start(f32[256,256]{1,0:T(8,128)} %get-tuple-element.559) | copy-start | bytes 786436
  545.0 52.9 %copy-start.4 = (f32[256,256]{1,0:T(8,128)S(1)}, f32[256,256]{1,0:T(8,128)}, u32[]{:S(2)}) copy-start(f32[256,256]{1,0:T(8,128)} %param.17) | copy-start | bytes 786436
  596.2 1.1 copy-start.22
  598.6 1.8 copy-start.8
  (13 other events, 9.2 us)
Sparse Core Ops, SparseCore 0:
  106.5 58.7 all-reduce.9
  276.4 266.3 all-reduce.5
  546.7 49.4 all-reduce.7
where the time goes:
time: 609 us; the launch traced here: 608 us
  waiting for transfers between devices  383 us (63%)
  other arithmetic  158 us (26%)
  local copies, waits for them, and re-layouts  38.7 us (6%)
  between operations  14.1 us (2%)
  matrix products  9.56 us (2%)
    psum x1, waiting for transfers between devices, body(): operator_total = operator_total + lax.psum(operator_grad, ('blk', 'rep'))  263 us
    psum x2, waiting for transfers between devices, body(): left_sum, right_sum = lax.psum((left_grad, right_grad), 'rep')  108 us
    scatter-add x4, other arithmetic, step(): table_grad = table_grad.at[rel_row, src_row].add(query_grad)  104 us
    scatter-add x8, other arithmetic, step(): right_grad = right_grad.at[neg_row].add(neg_grad).at[dst_row].add(pos_grad)  28.1 us
    gather x4, local copies, waits for them, and re-layouts, batch_terms(): queries = query_table[rel_row, src_row]  12.7 us
  transfers between devices with their start and end apart: 5, of which 4 were waited for; matrix products, arithmetic and copies ran while one was open for 1% of the time, Pallas kernels for 0%

commit v1 on v0

--- a/solution.py
+++ b/solution.py
@@ -1,9 +1,19 @@
+import functools
 import jax
 import jax.numpy as jnp
 from jax import lax
 from jax.sharding import PartitionSpec as P
 
 learn_rate = 0.1
+
+
+def show_local_data(in_array, axis_name, comm_axis):
+    for b in (axis_name, comm_axis):
+        in_array = lax.psum(in_array, b)
+    return in_array
+
+
+spread_the_loads = functools.partial(show_local_data, axis_name="rep", comm_axis="blk")
 
 
 def from_behind(block, axis, distance):
@@ -98,7 +108,7 @@
         left_grad, right_grad, operator_grad = bucket_terms(
             left_rows, right_rows, operator_bf, sources, targets, relations, negs, live_flags
         )
-        operator_total = operator_total + lax.psum(operator_grad, ("blk", "rep"))
+        operator_total = operator_total + spread_the_loads(operator_grad)
         left_sum, right_sum = lax.psum((left_grad, right_grad), "rep")
         left_rows, left_accum = row_update(left_rows, left_accum, left_sum)
         right_rows, right_accum = row_update(right_rows, right_accum, right_sum)

time: 609 us -> 1430 us (2.35)
  the two profiles are of different devices: /device:TPU:1 before, /device:TPU:2 now
where the time goes in v1:
time: 1430 us
  waiting for transfers between devices  1200 us (84%)
  other arithmetic  156 us (11%)
  local copies, waits for them, and re-layouts  40.5 us (3%)
    psum x1, waiting for transfers between devices, show_local_data(): in_array = lax.psum(in_array, b)  1090 us
    psum x2, waiting for transfers between devices, body(): left_sum, right_sum = lax.psum((left_grad, right_grad), 'rep')  106 us
    scatter-add x4, other arithmetic, step(): table_grad = table_grad.at[rel_row, src_row].add(query_grad)  104 us
  transfers between devices with their start and end apart: 5, of which 4 were waited for; matrix products, arithmetic and copies ran while one was open for 0% of the time, Pallas kernels for 0%

profile of v1, /device:TPU:2, one launch (start us, length us, event | category | flops | bytes accessed | tf_op | source)
XLA Modules:
  0.0 1429.7 jit_solution(7705722881691160842)
XLA Ops:
  14.2 91.4 %while.34 = (s32[]{:T(128)}, f32[2,256,256]{2,1,0:T(8,128)S(1)}, f32[256,256]{1,0:T(8,128)S(1)}, s32[2,512]{1,0:T(2,128)}, s32[2,512]{1,0:T(2,128)}, /*index=5*/...) while((s32[]{:T(128)}, f32[2,256,256]{2,1,0:T(8,128)S(1)}, ...), condition=%wide.region_7.8_spmd, body=%wide.region_0.7_spmd.sunk | while | flops 406075392 | bytes 12953801 | solution.py:72
  20.8 3.2 gather_fusion
  26.4 26.1 %scatter_fusion = f32[2,256,256]{2,1,0:T(8,128)S(1)} fusion(f32[2,256,256]{2,1,0:T(8,128)S(1)} %get-tuple-element.765, s32[512]{0:T(512)S(1)} %bitcast.154, f32[512,256]{1,0:T(8,128)S(1)} %convolution_add_fusion.5), kind=kCustom, calls=%fused_computation.6.clone.1 | custom fusion | flops 131072 | bytes 1576960 | tf_op jit(solution)/shard_map/while/body/eval_jaxpr/scatter-add | solution.py:67
  52.8 3.4 scatter_fusion.1
  56.3 3.6 scatter_custom_fusion.19
  66.5 3.2 gather_fusion
  72.1 26.1 %scatter_fusion = f32[2,256,256]{2,1,0:T(8,128)S(1)} fusion(f32[2,256,256]{2,1,0:T(8,128)S(1)} %get-tuple-element.765, s32[512]{0:T(512)S(1)} %bitcast.154, f32[512,256]{1,0:T(8,128)S(1)} %convolution_add_fusion.5), kind=kCustom, calls=%fused_computation.6.clone.1 | custom fusion | flops 131072 | bytes 1576960 | tf_op jit(solution)/shard_map/while/body/eval_jaxpr/scatter-add | solution.py:67
  98.5 3.4 scatter_fusion.1
  101.9 3.6 scatter_custom_fusion.19
  108.3 55.1 %all-reduce.10.cloned.1.call-done = (f32[256,256]{1,0:T(8,128)}, f32[256,256]{1,0:T(8,128)}) async-done(((f32[256,256]{1,0:T(8,128)}, f32[256,256]{1,0:T(8,128)}), (f32[256,256]{1,0:T(8,128)}, f32[256,256]{1,0:T(8,128)})) %all-reduce.10.cloned.1.call-update) | async-done | bytes 524304 | tf_op jit(solution)/shard_map/psum | solution.py:112
  165.9 4.6 collective-permute-start
  171.1 5.3 collective-permute-done
  176.8 91.3 %while.35 = (s32[]{:T(128)}, f32[2,256,256]{2,1,0:T(8,128)S(1)}, f32[256,256]{1,0:T(8,128)S(1)}, s32[2,512]{1,0:T(2,128)}, s32[2,512]{1,0:T(2,128)}, /*index=5*/...) while((s32[]{:T(128)}, f32[2,256,256]{2,1,0:T(8,128)S(1)}, ...), condition=%wide.region_19.20_spmd, body=%wide.region_12.19_spmd.sunk | while | flops 406075392 | bytes 12921097 | solution.py:72
  183.3 3.2 gather_fusion.3
  189.0 26.1 %scatter_fusion.2 = f32[2,256,256]{2,1,0:T(8,128)S(1)} fusion(f32[2,256,256]{2,1,0:T(8,128)S(1)} %get-tuple-element.798, s32[512]{0:T(512)S(1)} %bitcast.155, f32[512,256]{1,0:T(8,128)S(1)} %convolution_add_fusion.6), kind=kCustom, calls=%fused_computation.9.clone.1 | custom fusion | flops 131072 | bytes 1576960 | tf_op jit(solution)/shard_map/while/body/eval_jaxpr/scatter-add | solution.py:67
  215.4 3.4 scatter_fusion.3
  218.9 3.6 scatter_custom_fusion.23
  228.9 3.2 gather_fusion.3
  234.7 26.1 %scatter_fusion.2 = f32[2,256,256]{2,1,0:T(8,128)S(1)} fusion(f32[2,256,256]{2,1,0:T(8,128)S(1)} %get-tuple-element.798, s32[512]{0:T(512)S(1)} %bitcast.155, f32[512,256]{1,0:T(8,128)S(1)} %convolution_add_fusion.6), kind=kCustom, calls=%fused_computation.9.clone.1 | custom fusion | flops 131072 | bytes 1576960 | tf_op jit(solution)/shard_map/while/body/eval_jaxpr/scatter-add | solution.py:67
  261.1 3.4 scatter_fusion.3
  264.5 3.6 scatter_custom_fusion.23
  271.1 5.2 collective-permute-start.1
  276.3 51.4 %all-reduce.8.cloned.1.call-done = (f32[256,256]{1,0:T(8,128)}, f32[256,256]{1,0:T(8,128)}, f32[2,256,256]{2,1,0:T(8,128)}) async-done(((f32[256,256]{1,0:T(8,128)}, f32[256,256]{1,0:T(8,128)}, f32[2,256,256]{2,1,0:T(8,128)}), (f32[256,256]{1,0:T(8,128)}, f32[256,256]{1,0:T(8,128)}, f32[2,256,256]{2,1,0:T(8,128)})) %all-reduce.8.cloned.1.call-update) | async-done | bytes 1048592 | tf_op jit(solution)/shard_map/psum | solution.py:112
  332.9 1088.1 %all-reduce.6.cloned.1.call-done = f32[2,256,256]{2,1,0:T(8,128)} async-done(((f32[2,256,256]{2,1,0:T(8,128)}), f32[2,256,256]{2,1,0:T(8,128)}) %all-reduce.6.cloned.1.call-update) | async-done | bytes 524304 | tf_op jit(solution)/shard_map/psum | solution.py:12
  (166 shorter events, 60.3 us)
Async XLA Ops:
  7.2 156.2 %all-reduce.10.cloned.1.call-start = ((), (), s32[]{:S(2)}) async-start(), calls=%async_computation.2 | async-start | bytes 1048576 | tf_op jit(solution)/shard_map/psum | solution.py:112
  10.7 1.1 copy-start.2
  14.2 1.3 copy-start.13
  56.3 3.6 copy-start.14
  59.9 1.3 copy-start.13
  101.9 3.6 copy-start.14
  106.5 221.1 %all-reduce.8.cloned.1.call-start = ((), (), s32[]{:S(2)}) async-start(), calls=%async_computation.1 | async-start | bytes 2097152 | tf_op jit(solution)/shard_map/psum | solution.py:112
  163.4 1.1 copy-start.10
  164.5 6.0 copy-start.15
  165.8 4.7 copy-start.23
  165.8 4.8 copy-start.3
  165.8 4.8 copy-start.5
  165.9 10.6 collective-permute-start
  218.9 3.6 copy-start.29
  264.5 3.6 copy-start.29
  268.1 1.0 copy-start
  268.2 1.1 copy-start.8
  270.4 1150.6 %all-reduce.6.cloned.1.call-start = ((), (), s32[]{:S(2)}) async-start(), calls=%async_computation | async-start | bytes 1048576 | tf_op jit(solution)/shard_map/psum | solution.py:12
  271.1 58.9 %collective-permute-start.1 = (f32[256]{0:T(256)S(1)}, f32[256]{0:T(256)S(1)}, u32[]{:S(2)}, u32[]{:S(2)}) collective-permute-start(f32[256]{0:T(256)S(1)} %copy-done.27), channel_id=1, source_target_pairs={{508,0},{0,4},{4,8},{8,12},{12,16},{16,20},{20,24},{24,28},{28,32}... | collective-permute-start | bytes 3080 | tf_op jit(solution)/shard_map/ppermute | solution.py:22
  327.6 0.9 copy-start.11
  327.7 2.2 copy-start.9
  330.6 1.1 copy-start.6
  332.1 1088.9 %copy-start.7 = (f32[2,256,256]{2,1,0:T(8,128)S(1)}, f32[2,256,256]{2,1,0:T(8,128)}, u32[]{:S(2)}) copy-start(f32[2,256,256]{2,1,0:T(8,128)} %param.19) | copy-start | bytes 1572868
  332.1 1088.9 %copy-start.12 = (f32[2,256,256]{2,1,0:T(8,128)S(1)}, f32[2,256,256]{2,1,0:T(8,128)}, u32[]{:S(2)}) copy-start(f32[2,256,256]{2,1,0:T(8,128)} %param.20) | copy-start | bytes 1572868
  (15 other events, 10.4 us)
Sparse Core Ops, SparseCore 0:
  106.6 56.6 all-reduce.9
  270.5 57.0 all-reduce.7
  330.8 1090.1 all-reduce.5
